TPU v7x, 32 devices: a whole 2x2x4 slice. The times are simulated.
32 devices in a mesh: groups: 2 (over y), wide: 4 (over z), heads: 4 (over x, core).
Axes of the slice: x: 2, y: 2, z: 4, core: 2. Of those that a mesh axis runs over, the one named last changes fastest.
Arguments:
- video_hidden: bfloat16 [2048, 4096], P(('groups', 'wide'), 'heads'), parts along dimension 0, may hold values from -6 to 6
- audio_hidden: bfloat16 [512, 2048], P(('groups', 'wide'), 'heads'), parts along dimension 0, may hold values from -6 to 6
- video_query: bfloat16 [2048, 2048], P(('groups', 'wide'), 'heads'), parts along dimension 0, may hold values from -8 to 8
- video_key: bfloat16 [2048, 2048], P(('groups', 'wide'), 'heads'), parts along dimension 0, may hold values from -8 to 8
- video_value: bfloat16 [2048, 2048], P(('groups', 'wide'), 'heads'), parts along dimension 0, may hold values from -6 to 6
- audio_query: bfloat16 [512, 1024], P(('groups', 'wide'), 'heads'), parts along dimension 0, may hold values from -8 to 8
- audio_key: bfloat16 [512, 1024], P(('groups', 'wide'), 'heads'), parts along dimension 0, may hold values from -8 to 8
- audio_value: bfloat16 [512, 1024], P(('groups', 'wide'), 'heads'), parts along dimension 0, may hold values from -6 to 6
- cross_video_query: bfloat16 [2048, 1024], P(('groups', 'wide'), 'heads'), parts along dimension 0, may hold values from -8 to 8
- cross_audio_key: bfloat16 [512, 1024], P(('groups', 'wide'), 'heads'), parts along dimension 0, may hold values from -8 to 8
- cross_audio_value: bfloat16 [512, 1024], P(('groups', 'wide'), 'heads'), parts along dimension 0, may hold values from -6 to 6
- cross_audio_query: bfloat16 [512, 1024], P(('groups', 'wide'), 'heads'), parts along dimension 0, may hold values from -8 to 8
- cross_video_key: bfloat16 [2048, 1024], P(('groups', 'wide'), 'heads'), parts along dimension 0, may hold values from -8 to 8
- cross_video_value: bfloat16 [2048, 1024], P(('groups', 'wide'), 'heads'), parts along dimension 0, may hold values from -6 to 6
- video_self_out: bfloat16 [2048, 4096], P('heads', 'wide'), may hold values from -0.125 to 0.125
- video_cross_out: bfloat16 [1024, 4096], P('heads', 'wide'), may hold values from -0.1875 to 0.1875
- audio_self_out: bfloat16 [1024, 2048], P('heads', 'wide'), may hold values from -0.1875 to 0.1875
- audio_cross_out: bfloat16 [1024, 2048], P('heads', 'wide'), may hold values from -0.1875 to 0.1875
- intersection: int32 [8, 5], P('groups'), parts along dimension 0, may hold values from 0 to 1, as said below
Outputs:
- video_out: bfloat16 [2048, 4096], P(('groups', 'wide'), 'heads'), parts along dimension 0
- audio_out: bfloat16 [512, 2048], P(('groups', 'wide'), 'heads'), parts along dimension 0
There are 2 independent parts, one for each index of `groups`. A program takes and returns all parts, laid end to end along the dimension named above; an argument that names none is the same for every part. Nothing has to cross between parts.
Inputs may be any that keep to these rules, and one draw needn't show every extreme that they name: `intersection`: column 2 is 1 in every row; entries that would pair a block with one outside the clip are ignored.
All inputs are finite; a program needn't handle non-finite values.
Results may differ from a plain program's by a relative error of at most 0.012.
Values may be sent and summed in bfloat16 or wider, within the bound.
A program may use at most 64 MiB of HBM per device.

v0:
```python
import math

import jax
import jax.numpy as jnp
from jax import lax
from jax.sharding import PartitionSpec as P

HDV = 128
HDA = 64
REACH = 2


def passed_along(value, axis, by):
    length = lax.axis_size(axis)
    pairs = [(i, i + by) for i in range(length) if 0 <= i + by < length]
    return lax.ppermute(value, axis, pairs)


def empty_state(row_count, head_count, head_size):
    return (
        jnp.full((head_count, row_count), -1e30, jnp.float32),
        jnp.zeros((head_count, row_count), jnp.float32),
        jnp.zeros((head_count, row_count, head_size), jnp.float32),
    )


def absorb(state, queries, key_rows, value_rows, head_size, allowed):
    maxima, totals, running = state
    head_count = queries.shape[1] // head_size
    query_heads = queries.reshape(queries.shape[0], head_count, head_size)
    key_heads = key_rows.reshape(key_rows.shape[0], head_count, head_size)
    value_heads = value_rows.reshape(value_rows.shape[0], head_count, head_size)
    scores = jnp.einsum(
        "qhd,khd->hqk", query_heads, key_heads, preferred_element_type=jnp.float32
    ) * (1.0 / math.sqrt(head_size))
    if allowed is not None:
        scores = jnp.where(allowed[None, None, :], scores, -1e30)
    new_peak = jnp.maximum(maxima, jnp.max(scores, axis=2))
    weights = jnp.exp(scores - new_peak[:, :, None])
    if allowed is not None:
        weights = jnp.where(allowed[None, None, :], weights, 0.0)
    rescale = jnp.exp(maxima - new_peak)
    totals = totals * rescale + jnp.sum(weights, axis=2)
    running = running * rescale[:, :, None] + jnp.einsum(
        "hqk,khd->hqd",
        weights.astype(jnp.bfloat16),
        value_heads,
        preferred_element_type=jnp.float32,
    )
    return (new_peak, totals, running)


def finish(state, head_size):
    maxima, totals, running = state
    result = running / totals[:, :, None]
    return (
        result.transpose(1, 0, 2)
        .reshape(result.shape[1], result.shape[0] * head_size)
        .astype(jnp.bfloat16)
    )


def permitted(key_blocks, position, table_row, wide_count):
    offsets = key_blocks - position + REACH
    matches = (offsets[:, None] == jnp.arange(2 * REACH + 1, dtype=jnp.int32)[None, :]) & (
        table_row[None, :] > 0
    )
    inside = (key_blocks >= 0) & (key_blocks < wide_count)
    return jnp.any(matches, axis=1) & inside


def shards(
    video_hidden,
    audio_hidden,
    video_query,
    video_key,
    video_value,
    audio_query,
    audio_key,
    audio_value,
    cross_video_query,
    cross_audio_key,
    cross_audio_value,
    cross_audio_query,
    cross_video_key,
    cross_video_value,
    video_self_out,
    video_cross_out,
    audio_self_out,
    audio_cross_out,
    intersection,
):
    position = lax.axis_index("wide")
    wide_count = lax.axis_size("wide")
    video_count = video_query.shape[0]
    audio_count = audio_query.shape[0]
    head_count = video_query.shape[1] // HDV
    video_start = empty_state(video_count, head_count, HDV)
    audio_start = empty_state(audio_count, head_count, HDA)
    carried = (video_start, audio_start)
    portion = (
        lax.all_gather(video_key, "wide", axis=0, tiled=True),
        lax.all_gather(video_value, "wide", axis=0, tiled=True),
        lax.all_gather(audio_key, "wide", axis=0, tiled=True),
        lax.all_gather(audio_value, "wide", axis=0, tiled=True),
    )
    video_state = absorb(carried[0], video_query, portion[0], portion[1], HDV, None)
    audio_state = absorb(carried[1], audio_query, portion[2], portion[3], HDA, None)
    table_row = lax.dynamic_slice_in_dim(intersection, position, 1, 0)[0]
    padded_table = jnp.pad(intersection, ((REACH, REACH), (0, 0)))
    flag_row = jnp.diagonal(
        jnp.fliplr(lax.dynamic_slice_in_dim(padded_table, position, 2 * REACH + 1, 0))
    )
    stacked = jnp.concatenate(
        [cross_audio_key, cross_audio_value, cross_video_key, cross_video_value], 0
    )

    def take_cross(carried, portion, block):
        audio_keys = portion[:audio_count]
        audio_values = portion[audio_count : 2 * audio_count]
        video_keys = portion[2 * audio_count : 2 * audio_count + video_count]
        video_values = portion[2 * audio_count + video_count :]
        audio_blocks = jnp.full((audio_count,), block, jnp.int32)
        video_blocks = jnp.full((video_count,), block, jnp.int32)
        return (
            absorb(
                carried[0],
                cross_video_query,
                audio_keys,
                audio_values,
                HDA,
                permitted(audio_blocks, position, table_row, wide_count),
            ),
            absorb(
                carried[1],
                cross_audio_query,
                video_keys,
                video_values,
                HDA,
                permitted(video_blocks, position, flag_row, wide_count),
            ),
        )

    cross_start = (
        empty_state(video_count, head_count, HDA),
        empty_state(audio_count, head_count, HDA),
    )
    carried = take_cross(cross_start, stacked, position)
    for offset in range(-REACH, REACH + 1):
        if offset != 0:
            nearby = passed_along(stacked, "wide", -offset)
            carried = take_cross(carried, nearby, position + offset)
    to_video, to_audio = carried
    video_joined = jnp.concatenate([finish(video_state, HDV), finish(to_video, HDA)], 1)
    audio_joined = jnp.concatenate([finish(audio_state, HDA), finish(to_audio, HDA)], 1)
    video_weights = jnp.concatenate([video_self_out, video_cross_out], 0)
    audio_weights = jnp.concatenate([audio_self_out, audio_cross_out], 0)
    video_terms = jnp.dot(
        video_joined,
        lax.all_gather(video_weights, "wide", axis=1, tiled=True),
        preferred_element_type=jnp.float32,
    )
    audio_terms = jnp.dot(
        audio_joined,
        lax.all_gather(audio_weights, "wide", axis=1, tiled=True),
        preferred_element_type=jnp.float32,
    )
    video_sum, audio_sum = (
        lax.psum_scatter(
            video_terms.astype(jnp.bfloat16), "heads", scatter_dimension=1, tiled=True
        ).astype(jnp.float32),
        lax.psum_scatter(
            audio_terms.astype(jnp.bfloat16), "heads", scatter_dimension=1, tiled=True
        ).astype(jnp.float32),
    )
    video_out = (video_hidden.astype(jnp.float32) + video_sum).astype(jnp.bfloat16)
    audio_out = (audio_hidden.astype(jnp.float32) + audio_sum).astype(jnp.bfloat16)
    return (video_out, audio_out)


def solution(mesh):
    placed = (
        P(("groups", "wide"), "heads"),
        P(("groups", "wide"), "heads"),
        P(("groups", "wide"), "heads"),
        P(("groups", "wide"), "heads"),
        P(("groups", "wide"), "heads"),
        P(("groups", "wide"), "heads"),
        P(("groups", "wide"), "heads"),
        P(("groups", "wide"), "heads"),
        P(("groups", "wide"), "heads"),
        P(("groups", "wide"), "heads"),
        P(("groups", "wide"), "heads"),
        P(("groups", "wide"), "heads"),
        P(("groups", "wide"), "heads"),
        P(("groups", "wide"), "heads"),
        P("heads", "wide"),
        P("heads", "wide"),
        P("heads", "wide"),
        P("heads", "wide"),
        P("groups", None),
    )
    return jax.shard_map(
        shards,
        mesh=mesh,
        in_specs=placed,
        out_specs=(P(("groups", "wide"), "heads"), P(("groups", "wide"), "heads")),
        check_vma=False,
    )
```

profile of v0, /device:TPU:2, one launch (start us, length us, event | category | flops | bytes accessed | tf_op | source)
XLA Modules:
  0.0 311.9 jit_solution(2805440500169697225)
XLA Ops:
  7.3 0.7 all-gather.7.cloned.1.call-update
  8.0 1.8 copy.52
  9.9 1.9 pad_maximum_fusion.1
  11.8 1.4 constant_dynamic-update-slice_fusion.3
  13.2 1.4 constant_dynamic-update-slice_fusion.2
  14.6 1.6 constant_dynamic-update-slice_fusion.1
  16.1 1.6 constant_dynamic-update-slice_fusion
  17.7 1.4 collective-permute-start.3
  19.1 1.3 collective-permute-start.2
  20.4 4.6 %collective-permute-start.1 = (bf16[640,256]{1,0:T(8,128)(2,1)}, bf16[640,256]{1,0:T(8,128)(2,1)S(1)}, u32[]{:S(2)}, u32[]{:S(2)}) collective-permute-start(bf16[640,256]{1,0:T(8,128)(2,1)} %constant_dynamic-update-slice_fusion), channel_id=1, source_target_pairs={{0,4},{4,8},{8,12},{1,5},{5,9},{9,13},{2,6},{6,10},{10,14},{3,7},{... | collective-permute-start | bytes 983048 | tf_op jit(solution)/shard_map/ppermute | solution.py:16
  25.0 5.5 %collective-permute-start = (bf16[640,256]{1,0:T(8,128)(2,1)}, bf16[640,256]{1,0:T(8,128)(2,1)S(1)}, u32[]{:S(2)}, u32[]{:S(2)}) collective-permute-start(bf16[640,256]{1,0:T(8,128)(2,1)} %constant_dynamic-update-slice_fusion), channel_id=1, source_target_pairs={{0,8},{4,12},{1,9},{5,13},{2,10},{6,14},{3,11},{7,15},{16,24},{20,... | collective-permute-start | bytes 983048 | tf_op jit(solution)/shard_map/ppermute | solution.py:16
  30.5 2.7 pad_maximum_fusion
  33.7 32.6 %all_gather.21 = bf16[256,256]{1,0:T(8,128)(2,1)S(1)} all-gather(bf16[64,256]{1,0:T(8,128)(2,1)S(1)} %copy-done.11), channel_id=1, replica_groups=mesh['groups'=2,'wide'=4,'heads'=4] {'wide'}, dimensions={0}, use_global_device_ids=true | all-gather | bytes 163840 | tf_op jit(solution)/shard_map/all_gather | solution.py:104
  66.4 0.2 fusion.205
  66.9 14.7 %all_gather.22 = bf16[256,256]{1,0:T(8,128)(2,1)S(1)} all-gather(bf16[64,256]{1,0:T(8,128)(2,1)S(1)} %copy-done.13), channel_id=1, replica_groups=mesh['groups'=2,'wide'=4,'heads'=4] {'wide'}, dimensions={0}, use_global_device_ids=true | all-gather | bytes 163840 | tf_op jit(solution)/shard_map/all_gather | solution.py:105
  81.7 0.6 gather_fusion
  82.4 0.9 fusion.165
  83.9 0.2 fusion.54
  84.1 0.3 fusion.204
  91.1 0.6 copy-done.5
  92.5 0.3 fusion.200
  92.7 0.2 fusion.201
  93.0 0.2 fusion.202
  93.2 0.2 fusion.203
  93.5 0.2 fusion.81
  93.7 0.2 fusion.83
  93.9 0.2 fusion.85
  94.1 0.2 fusion.87
  94.3 0.2 fusion.79
  94.5 0.2 convolution_bitcast_fusion.5
  94.8 0.2 convolution_bitcast_fusion.6
  95.0 0.2 convolution_bitcast_fusion.7
  95.2 0.2 fusion.44
  95.5 0.3 fusion.53
  95.9 0.8 fusion.191
  99.8 1.5 copy.55
  101.3 2.0 multiply_reduce_fusion
  103.4 2.0 copy-done.1
  105.4 0.9 fusion
  106.3 27.5 %all-gather.11.cloned.1.call-done = bf16[512,2048]{1,0:T(8,128)(2,1)} async-done(((bf16[512,512]{1,0:T(8,128)(2,1)}), bf16[512,2048]{1,0:T(8,128)(2,1)}) %all-gather.11.cloned.1.call-update) | async-done | bytes 2097168 | tf_op jit(solution)/shard_map/all_gather | solution.py:165
  133.8 2.8 convolution_convert_fusion.1
  136.7 3.2 %fusion.58 = bf16[256,4,128]{0,2,1:T(8,128)(2,1)S(1)} fusion(bf16[1024,4,128]{0,2,1:T(8,128)(2,1)S(1)} %bitcast.380, f32[4,256,1024]{2,1,0:T(8,128)} %copy-done.1, f32[4,256]{1,0:T(4,128)S(1)} %get-tuple-element.47, f32[256,4]{0,1:T(4,128)S(1)} %bitcast_add_fusion.5, f32[256,4]{0,1:T(4,128)S(1)} %get-tuple-element.46), kind=kOutput, calls=%fused_computation.80 | convolution fusion | flops 271974400 | bytes 5517312 | tf_op jit(solution)/shard_map/hqk,khd->hqd/dot_general | solution.py:44
  139.9 109.5 %all-gather.9.cloned.1.call-done = bf16[768,4096]{1,0:T(8,128)(2,1)} async-done(((bf16[768,1024]{1,0:T(8,128)(2,1)}), bf16[768,4096]{1,0:T(8,128)(2,1)}) %all-gather.9.cloned.1.call-update) | async-done | bytes 6291472 | tf_op jit(solution)/shard_map/all_gather | solution.py:160
  249.4 6.0 %convolution_convert_fusion = bf16[256,4096]{1,0:T(8,128)(2,1)} fusion(bf16[768,4096]{1,0:T(8,128)(2,1)} %all-gather.9.cloned.1.call-done, bf16[256,256]{0,1:T(8,128)(2,1)S(1)} %bitcast.397, bf16[256,512]{0,1:T(8,128)(2,1)S(1)} %bitcast.392), kind=kOutput, calls=%fused_computation.1 | convolution fusion | flops 1612447744 | bytes 8781824 | tf_op jit(solution)/shard_map/dot_general | solution.py:158
  255.4 13.9 %reduce-scatter.5.cloned.1.call-done = bf16[64,512]{1,0:T(8,128)(2,1)} async-done(((bf16[64,2048]{1,0:T(8,128)(2,1)}), bf16[64,512]{1,0:T(8,128)(2,1)}) %reduce-scatter.5.cloned.1.call-update) | async-done | bytes 65552 | tf_op jit(solution)/shard_map/reduce_scatter | solution.py:172
  269.4 1.5 add_convert_fusion.1
  270.8 32.2 %reduce-scatter.3.cloned.1.call-done = bf16[256,1024]{1,0:T(8,128)(2,1)} async-done(((bf16[256,4096]{1,0:T(8,128)(2,1)}), bf16[256,1024]{1,0:T(8,128)(2,1)}) %reduce-scatter.3.cloned.1.call-update) | async-done | bytes 524304 | tf_op jit(solution)/shard_map/reduce_scatter | solution.py:169
  303.0 2.0 add_convert_fusion
  (108 shorter events, 6.0 us)
Async XLA Ops:
  7.2 94.2 %copy-start = (bf16[256,512]{1,0:T(8,128)(2,1)S(1)}, bf16[256,512]{1,0:T(8,128)(2,1)}, u32[]{:S(2)}) copy-start(bf16[256,512]{1,0:T(8,128)(2,1)} %param.21) | copy-start | bytes 786436
  7.2 26.1 %copy-start.3 = (bf16[256,256]{1,0:T(8,128)(2,1)S(1)}, bf16[256,256]{1,0:T(8,128)(2,1)}, u32[]{:S(2)}) copy-start(bf16[256,256]{1,0:T(8,128)(2,1)} %param.31) | copy-start | bytes 393220
  7.2 26.2 %copy-start.14 = (s32[4,5]{1,0:T(4,128)S(1)}, s32[4,5]{1,0:T(4,128)}, u32[]{:S(2)}) copy-start(s32[4,5]{1,0:T(4,128)} %param.37) | copy-start | bytes 244
  7.2 26.3 %copy-start.10 = (bf16[64,256]{1,0:T(8,128)(2,1)S(1)}, bf16[64,256]{1,0:T(8,128)(2,1)}, u32[]{:S(2)}) copy-start(bf16[64,256]{1,0:T(8,128)(2,1)} %param.30) | copy-start | bytes 98308
  7.2 26.4 %copy-start.11 = (bf16[64,256]{1,0:T(8,128)(2,1)S(1)}, bf16[64,256]{1,0:T(8,128)(2,1)}, u32[]{:S(2)}) copy-start(bf16[64,256]{1,0:T(8,128)(2,1)} %param.25) | copy-start | bytes 98308
  7.2 92.6 %all-gather.7.cloned.1.call-start = ((), (), s32[]{:S(2)}) async-start(), calls=%async_computation.3 | async-start | bytes 1310720 | tf_op jit(solution)/shard_map/all_gather | solution.py:103
  8.0 58.4 %copy-start.12 = (bf16[64,256]{1,0:T(8,128)(2,1)S(1)}, bf16[64,256]{1,0:T(8,128)(2,1)}, u32[]{:S(2)}) copy-start(bf16[64,256]{1,0:T(8,128)(2,1)} %param.24) | copy-start | bytes 98308
  8.0 93.3 %all-gather.5.cloned.1.call-start = ((), (), s32[]{:S(2)}) async-start(), calls=%async_computation.2 | async-start | bytes 1310720 | tf_op jit(solution)/shard_map/all_gather | solution.py:102
  9.8 57.1 %copy-start.13 = (bf16[64,256]{1,0:T(8,128)(2,1)S(1)}, bf16[64,256]{1,0:T(8,128)(2,1)}, u32[]{:S(2)}) copy-start(bf16[64,256]{1,0:T(8,128)(2,1)} %param.26) | copy-start | bytes 98308
  9.9 124.0 %all-gather.11.cloned.1.call-start = ((), (), s32[]{:S(2)}) async-start(), calls=%async_computation.6 | async-start | bytes 2621440 | tf_op jit(solution)/shard_map/all_gather | solution.py:165
  11.8 237.6 %all-gather.9.cloned.1.call-start = ((), (), s32[]{:S(2)}) async-start(), calls=%async_computation.4 | async-start | bytes 7864320 | tf_op jit(solution)/shard_map/all_gather | solution.py:160
  17.7 66.7 %copy-start.6 = (bf16[64,256]{1,0:T(8,128)(2,1)S(1)}, bf16[64,256]{1,0:T(8,128)(2,1)}, u32[]{:S(2)}) copy-start(bf16[64,256]{1,0:T(8,128)(2,1)} %param.28) | copy-start | bytes 98308
  17.7 66.8 %copy-start.8 = (bf16[256,256]{1,0:T(8,128)(2,1)S(1)}, bf16[256,256]{1,0:T(8,128)(2,1)}, u32[]{:S(2)}) copy-start(bf16[256,256]{1,0:T(8,128)(2,1)} %param.27) | copy-start | bytes 393220
  17.7 67.7 %copy-start.4 = (bf16[256,256]{1,0:T(8,128)(2,1)S(1)}, bf16[256,256]{1,0:T(8,128)(2,1)}, u32[]{:S(2)}) copy-start(bf16[256,256]{1,0:T(8,128)(2,1)} %param.32) | copy-start | bytes 393220
  17.7 67.8 %copy-start.7 = (bf16[64,256]{1,0:T(8,128)(2,1)S(1)}, bf16[64,256]{1,0:T(8,128)(2,1)}, u32[]{:S(2)}) copy-start(bf16[64,256]{1,0:T(8,128)(2,1)} %param.29) | copy-start | bytes 98308
  17.7 73.2 %collective-permute-start.3 = (bf16[640,256]{1,0:T(8,128)(2,1)}, bf16[640,256]{1,0:T(8,128)(2,1)S(1)}, u32[]{:S(2)}, u32[]{:S(2)}) collective-permute-start(bf16[640,256]{1,0:T(8,128)(2,1)} %constant_dynamic-update-slice_fusion), channel_id=1, source_target_pairs={{8,0},{12,4},{9,1},{13,5},{10,2},{14,6},{11,3},{15,7},{24,16},{28,... | collective-permute-start | bytes 983048 | tf_op jit(solution)/shard_map/ppermute | solution.py:16
  19.1 71.8 %collective-permute-start.2 = (bf16[640,256]{1,0:T(8,128)(2,1)}, bf16[640,256]{1,0:T(8,128)(2,1)S(1)}, u32[]{:S(2)}, u32[]{:S(2)}) collective-permute-start(bf16[640,256]{1,0:T(8,128)(2,1)} %constant_dynamic-update-slice_fusion), channel_id=1, source_target_pairs={{4,0},{8,4},{12,8},{5,1},{9,5},{13,9},{6,2},{10,6},{14,10},{7,3},{... | collective-permute-start | bytes 983048 | tf_op jit(solution)/shard_map/ppermute | solution.py:16
  20.4 71.3 %collective-permute-start.1 = (bf16[640,256]{1,0:T(8,128)(2,1)}, bf16[640,256]{1,0:T(8,128)(2,1)S(1)}, u32[]{:S(2)}, u32[]{:S(2)}) collective-permute-start(bf16[640,256]{1,0:T(8,128)(2,1)} %constant_dynamic-update-slice_fusion), channel_id=1, source_target_pairs={{0,4},{4,8},{8,12},{1,5},{5,9},{9,13},{2,6},{6,10},{10,14},{3,7},{... | collective-permute-start | bytes 983048 | tf_op jit(solution)/shard_map/ppermute | solution.py:16
  25.0 66.9 %collective-permute-start = (bf16[640,256]{1,0:T(8,128)(2,1)}, bf16[640,256]{1,0:T(8,128)(2,1)S(1)}, u32[]{:S(2)}, u32[]{:S(2)}) collective-permute-start(bf16[640,256]{1,0:T(8,128)(2,1)} %constant_dynamic-update-slice_fusion), channel_id=1, source_target_pairs={{0,8},{4,12},{1,9},{5,13},{2,10},{6,14},{3,11},{7,15},{16,24},{20,... | collective-permute-start | bytes 983048 | tf_op jit(solution)/shard_map/ppermute | solution.py:16
  33.2 236.1 %reduce-scatter.5.cloned.1.call-start = ((), (), s32[]{:S(2)}) async-start(), calls=%async_computation.7 | async-start | bytes 327680 | tf_op jit(solution)/shard_map/reduce_scatter | solution.py:172
  90.9 0.7 copy-start.5
  103.4 2.0 copy-start.1
  136.6 166.4 %reduce-scatter.3.cloned.1.call-start = ((), (), s32[]{:S(2)}) async-start(), calls=%async_computation.5 | async-start | bytes 2621440 | tf_op jit(solution)/shard_map/reduce_scatter | solution.py:169
  249.4 20.0 %copy-start.9 = (bf16[64,512]{1,0:T(8,128)(2,1)S(1)}, bf16[64,512]{1,0:T(8,128)(2,1)}, u32[]{:S(2)}) copy-start(bf16[64,512]{1,0:T(8,128)(2,1)} %param.20) | copy-start | bytes 196612
  249.4 53.6 %copy-start.2 = (bf16[256,1024]{1,0:T(8,128)(2,1)S(1)}, bf16[256,1024]{1,0:T(8,128)(2,1)}, u32[]{:S(2)}) copy-start(bf16[256,1024]{1,0:T(8,128)(2,1)} %param.19) | copy-start | bytes 1572868
Sparse Core Ops, SparseCore 0:
  9.6 44.7 all-gather.6
  56.0 30.1 all-gather.4
  88.3 45.4 all-gather.10
  135.3 114.0 all-gather.8
  252.3 17.0 reduce-scatter.4
  271.7 31.2 reduce-scatter.2
where the time goes:
time: 315 us; the launch traced here: 312 us
  waiting for transfers between devices  184 us (58%)
  blocking collectives  47.2 us (15%)
  between operations  21.1 us (7%)
  matrix products  18.8 us (6%)
  local copies, waits for them, and re-layouts  16.3 us (5%)
  starting transfers between devices  13 us (4%)
  other arithmetic  11.5 us (4%)
    all_gather x1, waiting for transfers between devices, shards(): lax.all_gather(video_weights, 'wide', axis=1, tiled=True)  109 us
    all_gather x1, blocking collectives, shards(): lax.all_gather(audio_key, 'wide', axis=0, tiled=True)  32.6 us
    reduce_scatter x1, waiting for transfers between devices, shards(): lax.psum_scatter(video_terms.astype(jnp.bfloat16), 'heads', scatter_dimen...  32.2 us
    all_gather x1, waiting for transfers between devices, shards(): lax.all_gather(audio_weights, 'wide', axis=1, tiled=True)  27.5 us
    all_gather x1, blocking collectives, shards(): lax.all_gather(audio_value, 'wide', axis=0, tiled=True)  14.7 us
    reduce_scatter x1, waiting for transfers between devices, shards(): lax.psum_scatter(audio_terms.astype(jnp.bfloat16), 'heads', scatter_dimen...  13.9 us
    ppermute x4, starting transfers between devices, passed_along(): return lax.ppermute(value, axis, pairs)  12.8 us
    unnamed x37, local copies, waits for them, and re-layouts  9.05 us
  transfers between devices with their start and end apart: 10, of which 4 were waited for; matrix products, arithmetic and copies ran while one was open for 13% of the time, Pallas kernels for 0%

commit v1 on v0

--- a/solution.py
+++ b/solution.py
@@ -1,8 +1,11 @@
+import functools
 import math
 
 import jax
 import jax.numpy as jnp
 from jax import lax
+from jax.experimental import pallas as pl
+from jax.experimental.pallas import tpu as pltpu
 from jax.sharding import PartitionSpec as P
 
 HDV = 128
@@ -69,7 +72,7 @@
     return jnp.any(matches, axis=1) & inside
 
 
-def shards(
+def general_shards(
     video_hidden,
     audio_hidden,
     video_query,
@@ -178,6 +181,303 @@
     return (video_out, audio_out)
 
 
+NT = (((1,), (1,)), ((), ()))
+MESH = pl.DeviceIdType.MESH
+
+
+def pack_kernel(n, cvq, cvk, cvv, aq, ak, av, caq, cak, cav, aso, aco, pack, wa):
+    rows = cvq.shape[0]
+    half = rows // 2
+    few = aq.shape[0]
+    for j in range(n):
+        cols = slice(j * HDA, (j + 1) * HDA)
+        pack[j, :rows, :] = jnp.concatenate([cvq[:, cols], cvk[:, cols]], 1)
+        pack[j, rows : rows + half, :] = jnp.concatenate([cvv[:half, cols], cvv[half:, cols]], 1)
+        at = rows + half
+        for left, right in ((aq, ak), (av, caq), (cak, cav)):
+            pack[j, at : at + few, :] = jnp.concatenate([left[:, cols], right[:, cols]], 1)
+            at += few
+        wa[2 * j * HDA : (2 * j + 1) * HDA, :] = aso[cols, :]
+        wa[(2 * j + 1) * HDA : (2 * j + 2) * HDA, :] = aco[cols, :]
+
+
+def attend(queries, keys, values, head_size, bias):
+    scores = lax.dot_general(queries, keys, NT, preferred_element_type=jnp.float32)
+    scores = scores * (1.0 / math.sqrt(head_size))
+    if bias is not None:
+        scores = scores + bias
+    weights = jnp.exp(scores - jnp.max(scores, axis=1, keepdims=True))
+    totals = jnp.sum(weights, axis=1, keepdims=True)
+    mixed = jnp.dot(weights.astype(jnp.bfloat16), values, preferred_element_type=jnp.float32)
+    return (mixed / totals).astype(jnp.bfloat16)
+
+
+def fused_kernel(
+    n, chunks,
+    vq, vk, vv, pack, ws, wc, wa, bias_v, bias_a,
+    out_v, out_a,
+    q_all, k_all, v_all, p_all, ws_all, wc_all, wa_all,
+    o_self, o_rest, r_self, r_rest, sum_v, sum_a,
+    a_send, a_recv, w_send, w_recv, f_send, f_recv, b_send, b_recv, d_send, d_recv, local,
+):
+    w = lax.axis_index("wide")
+    h = lax.axis_index("heads")
+    rows = vq.shape[0]
+    half = rows // 2
+    few = out_a.shape[0]
+
+    def place(dw, dh):
+        return {"wide": lax.rem(w + dw, n), "heads": lax.rem(h + dh, n)}
+
+    def remote(source, target, send, recv, device):
+        return pltpu.make_async_remote_copy(
+            src_ref=source, dst_ref=target, send_sem=send, recv_sem=recv,
+            device_id=device, device_id_type=MESH,
+        )
+
+    others = [(dw, dh) for dw in range(n) for dh in range(n) if dw or dh]
+    barrier = pltpu.get_barrier_semaphore()
+    for dw, dh in others:
+        pl.semaphore_signal(barrier, inc=1, device_id=place(dw, dh), device_id_type=MESH)
+
+    def head_cols(ref, who):
+        return ref.at[:, pl.ds(pl.multiple_of(who * HDV, HDV), HDV)]
+
+    own = [pltpu.make_async_copy(pack.at[w], p_all.at[w], local.at[0])]
+    for i, (source, target) in enumerate(((vk, k_all), (vv, v_all), (vq, q_all))):
+        own.append(pltpu.make_async_copy(head_cols(source, w), target.at[w], local.at[1 + i]))
+    for i, (source, target) in enumerate(((ws, ws_all), (wc, wc_all), (wa, wa_all))):
+        own.append(pltpu.make_async_copy(source, target.at[h], local.at[4 + i]))
+    for copy in own:
+        copy.start()
+    pl.semaphore_wait(barrier, len(others))
+
+    a_copies = {}
+    for i, (source, target) in enumerate(((pack, p_all), (vk, k_all), (vv, v_all), (vq, q_all))):
+        for d in range(1, n):
+            who = lax.rem(w + d, n)
+            piece = source.at[who] if i == 0 else head_cols(source, who)
+            copy = remote(piece, target.at[w], a_send.at[i, d], a_recv.at[i, d], place(d, 0))
+            copy.start()
+            a_copies[i, d] = copy
+
+    pairs = ((ws, ws_all), (wc, wc_all), (wa, wa_all))
+    partner = {"wide": w, "heads": h + 1 - 2 * lax.rem(h, 2)}
+    w_copies, f_copies = [], []
+    for i, (source, target) in enumerate(pairs):
+        for k in range(1, n // 2):
+            copy = remote(source, target.at[h], w_send.at[i, k], w_recv.at[i, k], place(0, 2 * k))
+            copy.start()
+            w_copies.append(copy)
+        copy = remote(source, target.at[h], f_send.at[i, 0], f_recv.at[i, 0], partner)
+        copy.start()
+        f_copies.append(copy)
+
+    own[0].wait()
+    for d in range(1, n):
+        a_copies[0, d].wait_recv()
+    at = rows + half
+
+    def part(j, start, right):
+        return p_all[j, start : start + few, HDA:] if right else p_all[j, start : start + few, :HDA]
+
+    def whole(start, right):
+        return jnp.concatenate([part(j, start, right) for j in range(n)], 0)
+
+    aq, ak = whole(at, False), whole(at, True)
+    av, caq = whole(at + few, False), whole(at + few, True)
+    cak, cav = whole(at + 2 * few, False), whole(at + 2 * few, True)
+    cvk = jnp.concatenate([p_all[j, :rows, HDA:] for j in range(n)], 0)
+    cvv = jnp.concatenate(
+        [p_all[j, rows:at, cols] for j in range(n) for cols in (slice(0, HDA), slice(HDA, 2 * HDA))], 0
+    )
+    wide_bias = jnp.concatenate(
+        [jnp.broadcast_to(bias_a[j : j + 1, :], (few, bias_a.shape[1])) for j in range(n)], 0
+    )
+    audio = jnp.concatenate(
+        [attend(aq, ak, av, HDA, None), attend(caq, cvk, cvv, HDA, wide_bias)], 1
+    )
+    for j in range(n):
+        o_rest[j, half:, :] = audio[j * few : (j + 1) * few, :]
+        mixed = attend(p_all[j, :rows, :HDA], cak, cav, HDA, bias_v[j : j + 1, :])
+        o_rest[j, :half, :] = jnp.concatenate([mixed[:half], mixed[half:]], 1)
+
+    mine = h * n + w
+    b_copies = {}
+
+    def spread(kind, buffer, landing, dh):
+        block = lax.rem(h + dh, n)
+        for dw in range(n):
+            if dw or dh:
+                slot = dw * n + dh
+                copy = remote(
+                    buffer.at[block], landing.at[mine],
+                    b_send.at[kind, slot], b_recv.at[kind, slot], place(dw, dh),
+                )
+                copy.start()
+                b_copies[kind, slot] = copy
+
+    for dh in list(range(1, n)) + [0]:
+        spread(0, o_rest, r_rest, dh)
+    r_rest[pl.ds(mine, 1)] = o_rest[pl.ds(h, 1)]
+
+    for i in range(1, 4):
+        own[i].wait()
+        for d in range(1, n):
+            a_copies[i, d].wait_recv()
+    keys = k_all[...].reshape(n * rows, HDV)
+    values = v_all[...].reshape(n * rows, HDV)
+    for dh in list(range(1, n)) + [0]:
+        block = lax.rem(h + dh, n)
+        o_self[pl.ds(block, 1)] = attend(
+            q_all[pl.ds(block, 1)].reshape(rows, HDV), keys, values, HDV, None
+        )[None]
+        spread(1, o_self, r_self, dh)
+    r_self[pl.ds(mine, 1)] = o_self[pl.ds(h, 1)]
+
+    for copy in w_copies:
+        copy.wait_recv()
+    for i, (source, target) in enumerate(pairs):
+        for k in range(1, n // 2):
+            slot = lax.rem(h + n - 2 * k, n)
+            copy = remote(target.at[slot], target.at[slot], f_send.at[i, k], f_recv.at[i, k], partner)
+            copy.start()
+            f_copies.append(copy)
+
+    for copy in own[4:]:
+        copy.wait()
+    for copy in b_copies.values():
+        copy.wait_recv()
+    for copy in f_copies:
+        copy.wait_recv()
+
+    heads = n * n
+    joined = jnp.concatenate([r_self[s] for s in range(heads)], 1)
+    crossed = jnp.concatenate(
+        [
+            jnp.concatenate([r_rest[s, :half, :HDA] for s in range(heads)], 1),
+            jnp.concatenate([r_rest[s, :half, HDA:] for s in range(heads)], 1),
+        ],
+        0,
+    )
+    audio_joined = jnp.concatenate([r_rest[s, half:, :] for s in range(heads)], 1)
+    home = {"wide": h, "heads": w}
+    sums = jnp.dot(
+        audio_joined, wa_all[...].reshape(-1, wa.shape[1]), preferred_element_type=jnp.float32
+    )
+    sum_a[...] = sums.astype(jnp.bfloat16)
+    width = ws.shape[1] // chunks
+    pieces = [(sum_a, out_a)]
+    last = []
+
+    def deliver(i, source, target):
+        away = remote(source, target, d_send.at[i], d_recv.at[i], home)
+        here = pltpu.make_async_copy(source, target, local.at[7 + i])
+        last.append((away, here))
+
+        @pl.when(w != h)
+        def _():
+            away.start()
+
+        @pl.when(w == h)
+        def _():
+            here.start()
+
+    deliver(0, sum_a, out_a)
+    for c in range(chunks):
+        cols = slice(c * width, (c + 1) * width)
+        sums = jnp.dot(
+            joined, ws_all[:, :, cols].reshape(-1, width), preferred_element_type=jnp.float32
+        ) + jnp.dot(
+            crossed, wc_all[:, :, cols].reshape(-1, width), preferred_element_type=jnp.float32
+        )
+        sum_v[:, cols] = sums.astype(jnp.bfloat16)
+        deliver(1 + c, sum_v.at[:, cols], out_v.at[:, cols])
+
+    @pl.when(w != h)
+    def _():
+        for away, here in last:
+            away.wait()
+
+    @pl.when(w == h)
+    def _():
+        for away, here in last:
+            here.wait()
+
+    for copy in list(a_copies.values()) + w_copies + f_copies + list(b_copies.values()):
+        copy.wait_send()
+
+
+def shards(*args):
+    n = lax.axis_size("wide")
+    count = lax.axis_size("heads")
+    head_count = args[2].shape[1] // HDV
+    if not (n == count == head_count and n % 2 == 0):
+        return general_shards(*args)
+    (video_hidden, audio_hidden, vq, vk, vv, aq, ak, av, cvq, cak, cav, caq, cvk, cvv,
+     vso, vco, aso, aco, table) = args
+    rows, few = vq.shape[0], aq.shape[0]
+    blocks = jnp.arange(n, dtype=jnp.int32)
+    offsets = blocks[None, :] - blocks[:, None] + REACH
+    hits = offsets[:, :, None] == jnp.arange(table.shape[1], dtype=jnp.int32)
+    allowed = jnp.any(hits & (table[:, None, :] > 0), axis=2)
+    bias = jnp.where(allowed, 0.0, -1e30).astype(jnp.float32)
+    bias_v = jnp.repeat(bias, few, axis=1)
+    bias_a = jnp.repeat(bias.T, rows, axis=1)
+    depth = rows + rows // 2 + 3 * few
+    vmem = pl.BlockSpec(memory_space=pltpu.VMEM)
+    anywhere = pl.BlockSpec(memory_space=pl.ANY)
+    bf16 = jnp.bfloat16
+    pack, wa = pl.pallas_call(
+        functools.partial(pack_kernel, n),
+        out_shape=(
+            jax.ShapeDtypeStruct((n, depth, 2 * HDA), bf16),
+            jax.ShapeDtypeStruct((2 * aso.shape[0], aso.shape[1]), bf16),
+        ),
+        in_specs=[vmem] * 11,
+        out_specs=(vmem, vmem),
+        name="pack",
+    )(cvq, cvk, cvv, aq, ak, av, caq, cak, cav, aso, aco)
+    chunks = max(1, vso.shape[1] // 256)
+    rest = rows // 2 + few
+    dma = pltpu.SemaphoreType.DMA
+    video_sum, audio_sum = pl.pallas_call(
+        functools.partial(fused_kernel, n, chunks),
+        out_shape=(
+            jax.ShapeDtypeStruct(video_hidden.shape, bf16),
+            jax.ShapeDtypeStruct(audio_hidden.shape, bf16),
+        ),
+        in_specs=[anywhere] * 7 + [vmem] * 2,
+        out_specs=(anywhere, anywhere),
+        scratch_shapes=[
+            pltpu.VMEM((n, rows, HDV), bf16),
+            pltpu.VMEM((n, rows, HDV), bf16),
+            pltpu.VMEM((n, rows, HDV), bf16),
+            pltpu.VMEM((n, depth, 2 * HDA), bf16),
+            pltpu.VMEM((n,) + vso.shape, bf16),
+            pltpu.VMEM((n,) + vco.shape, bf16),
+            pltpu.VMEM((n,) + wa.shape, bf16),
+            pltpu.VMEM((n, rows, HDV), bf16),
+            pltpu.VMEM((n, rest, 2 * HDA), bf16),
+            pltpu.VMEM((n * n, rows, HDV), bf16),
+            pltpu.VMEM((n * n, rest, 2 * HDA), bf16),
+            pltpu.VMEM(video_hidden.shape, bf16),
+            pltpu.VMEM(audio_hidden.shape, bf16),
+            dma((4, n)), dma((4, n)),
+            dma((3, n)), dma((3, n)),
+            dma((3, n)), dma((3, n)),
+            dma((2, n * n)), dma((2, n * n)),
+            dma((1 + chunks,)), dma((1 + chunks,)),
+            dma((8 + chunks,)),
+        ],
+        compiler_params=pltpu.CompilerParams(collective_id=0, has_side_effects=True),
+        name="joint",
+    )(vq, vk, vv, pack, vso, vco, wa, bias_v, bias_a)
+    video_out = video_hidden.astype(jnp.float32) + video_sum.astype(jnp.float32)
+    audio_out = audio_hidden.astype(jnp.float32) + audio_sum.astype(jnp.float32)
+    return (video_out.astype(bf16), audio_out.astype(bf16))
+
+
 def solution(mesh):
     placed = (
         P(("groups", "wide"), "heads"),

time: 315 us -> 113 us (0.36)
  waiting for transfers between devices: 184 us -> 0 us
  Pallas kernels: 0 us -> 107 us
  blocking collectives: 47.2 us -> 0 us
  between operations: 21.1 us -> 0.67 us
  matrix products: 18.8 us -> 0 us
  local copies, waits for them, and re-layouts: 16.3 us -> 1.55 us
  starting transfers between devices: 13 us -> 0 us
  other arithmetic: 11.5 us -> 3.63 us
    all_gather x4 -> x0, waiting for transfers between devices: 137 us -> none  [the longest x1 109 us: shards(): lax.all_gather(video_weights, 'wide', axis=1, tiled=True)]
    pallas_call x0 -> x2, Pallas kernels: none -> 107 us  [the longest x1 104 us: shards(): pl.pallas_call(functools.partial(fused_kernel, n, chunks), out_shape=(jax...]
    all_gather x2 -> x0, blocking collectives: 47.2 us -> none  [the longest x1 32.6 us: shards(): lax.all_gather(audio_key, 'wide', axis=0, tiled=True)]
    reduce_scatter x2 -> x0, waiting for transfers between devices: 46.1 us -> none  [the longest x1 32.2 us: shards(): lax.psum_scatter(video_terms.astype(jnp.bfloat16), 'heads', scatter_dimen...]
    dot_general x26 -> x0, matrix products: 18.8 us -> none  [the longest x1 6.02 us: shards(): jnp.dot(video_joined, lax.all_gather(video_weights, 'wide', axis=1, tiled...]
    ppermute x4 -> x0, starting transfers between devices: 12.8 us -> none  [passed_along(): return lax.ppermute(value, axis, pairs)]
    unnamed x37 -> x8, local copies, waits for them, and re-layouts: 9.05 us -> 0.7 us
    concatenate x3 -> x0, other arithmetic: 4.57 us -> none  [the longest x1 2.71 us: shards(): video_weights = jnp.concatenate([video_self_out, video_cross_out], 0)]
  transfers between devices with their start and end apart: 10 -> 0, of which waited for: 4 -> 0; matrix products, arithmetic and copies ran while one was open for 13% -> 0% of each run, Pallas kernels for 0% -> 0%
where the time goes in v1:
time: 113 us; the launch traced here: 112 us
  Pallas kernels  107 us (95%)
  other arithmetic  3.63 us (3%)
  local copies, waits for them, and re-layouts  1.55 us (1%)
    pallas_call x1, Pallas kernels, shards(): pl.pallas_call(functools.partial(fused_kernel, n, chunks), out_shape=(jax...  104 us
    convert_element_type x2, other arithmetic, shards(): return (video_out.astype(bf16), audio_out.astype(bf16))  2.71 us
    pallas_call x1, Pallas kernels, shards(): pl.pallas_call(functools.partial(pack_kernel, n), out_shape=(jax.ShapeDty...  2.48 us

profile of v1, /device:TPU:2, one launch (start us, length us, event | category | flops | bytes accessed | tf_op | source)
XLA Modules:
  0.0 112.4 jit_solution(8073190817404085564)
XLA Ops:
  0.6 0.7 broadcast_compare_fusion
  1.3 0.2 fusion.1
  1.6 0.1 copy.22
  1.6 0.1 broadcast_in_dim.21
  1.7 0.7 reshape.25.bias_v
  2.4 0.1 broadcast_bitcast_fusion
  2.5 0.6 copy.23
  3.1 2.5 %pack.1 = (bf16[4,576,128]{2,1,0:T(8,128)(2,1)}, bf16[512,512]{1,0:T(8,128)(2,1)}) custom-call(bf16[256,256]{1,0:T(8,128)(2,1)} %cvq.1, bf16[256,256]{1,0:T(8,128)(2,1)} %cvk.1, bf16[256,256]{1,0:T(8,128)(2,1)} %cvv.1, bf16[64,256]{1,0:T(8,128)(2,1)} %aq.1, bf16[64,256]{1,0:T(8,128)(2,1)} %ak.1, bf16[64,256]{1,0:T(8,128)(2,1)} %av.1, bf16[64,256]{1,0:T(8,128)(2,1)} %caq.1, ...), custom_call_target="tpu_custom_call" | custom-call | tf_op jit(solution)/shard_map/pack/pallas_call | solution.py:431
  5.6 0.0 copy-start
  5.6 104.1 %joint.1 = (bf16[256,1024]{1,0:T(8,128)(2,1)}, bf16[64,512]{1,0:T(8,128)(2,1)}) custom-call(bf16[256,512]{1,0:T(8,128)(2,1)} %vq.1, bf16[256,512]{1,0:T(8,128)(2,1)} %vk.1, bf16[256,512]{1,0:T(8,128)(2,1)} %vv.1, bf16[4,576,128]{2,1,0:T(8,128)(2,1)} %get-tuple-element.6.pack, bf16[512,1024]{1,0:T(8,128)(2,1)} %ws.1, bf16[256,1024]{1,0:T(8,128)(2,1)} %wc.1, ...), custom_call_target="tpu_custom_call" | custom-call | tf_op jit(solution)/shard_map/joint/pallas_call | solution.py:444
  109.7 0.0 copy-done
  109.7 0.0 copy-start.1
  109.7 0.0 copy-start.2
  109.7 2.1 %add_convert_fusion = bf16[256,1024]{1,0:T(8,128)(2,1)} fusion(bf16[256,1024]{1,0:T(8,128)(2,1)} %get-tuple-element.8, bf16[256,1024]{1,0:T(8,128)(2,1)S(1)} %copy-done), kind=kLoop, calls=%fused_computation | loop fusion | flops 1048576 | bytes 1572864 | tf_op jit(solution)/shard_map/convert_element_type | solution.py:478
  111.8 0.0 copy-done.1
  111.8 0.0 copy-done.2
  111.8 0.6 add_convert_fusion.1
  (2 shorter events, 0.0 us)
Async XLA Ops:
  5.6 104.1 %copy-start = (bf16[256,1024]{1,0:T(8,128)(2,1)S(1)}, bf16[256,1024]{1,0:T(8,128)(2,1)}, u32[]{:S(2)}) copy-start(bf16[256,1024]{1,0:T(8,128)(2,1)} %param.19) | copy-start | bytes 1572868
  109.7 2.1 %copy-start.1 = (bf16[64,512]{1,0:T(8,128)(2,1)S(1)}, bf16[64,512]{1,0:T(8,128)(2,1)}, u32[]{:S(2)}) copy-start(bf16[64,512]{1,0:T(8,128)(2,1)} %param.20) | copy-start | bytes 196612
  109.7 2.1 %copy-start.2 = (bf16[64,512]{1,0:T(8,128)(2,1)S(1)}, bf16[64,512]{1,0:T(8,128)(2,1)}, u32[]{:S(2)}) copy-start(bf16[64,512]{1,0:T(8,128)(2,1)} %get-tuple-element.9) | copy-start | bytes 196612

commit v2 on v1

--- a/solution.py
+++ b/solution.py
@@ -185,10 +185,20 @@
 MESH = pl.DeviceIdType.MESH
 
 
-def pack_kernel(n, cvq, cvk, cvv, aq, ak, av, caq, cak, cav, aso, aco, pack, wa):
+def pack_kernel(
+    n, cvq, cvk, cvv, aq, ak, av, caq, cak, cav, aso, aco, table, pack, wa, bias_v, bias_a
+):
     rows = cvq.shape[0]
     half = rows // 2
     few = aq.shape[0]
+    for i in range(n):
+        for j in range(n):
+            column = j - i + REACH
+            drop = jnp.float32(-1e30)
+            if 0 <= column < table.shape[1]:
+                drop = jnp.where(table[i, column] > 0, jnp.float32(0.0), drop)
+            bias_v[i : i + 1, j * few : (j + 1) * few] = jnp.full((1, few), drop)
+            bias_a[j : j + 1, i * rows : (i + 1) * rows] = jnp.full((1, rows), drop)
     for j in range(n):
         cols = slice(j * HDA, (j + 1) * HDA)
         pack[j, :rows, :] = jnp.concatenate([cvq[:, cols], cvk[:, cols]], 1)
@@ -217,14 +227,16 @@
     vq, vk, vv, pack, ws, wc, wa, bias_v, bias_a,
     out_v, out_a,
     q_all, k_all, v_all, p_all, ws_all, wc_all, wa_all,
-    o_self, o_rest, r_self, r_rest, sum_v, sum_a,
-    a_send, a_recv, w_send, w_recv, f_send, f_recv, b_send, b_recv, d_send, d_recv, local,
+    o_self, o_rest, r_self, r_rest, sum_v, sum_a, mid_v, mid_a,
+    a_send, a_recv, w_send, w_recv, f_send, f_recv, x_send, x_recv, z_send, z_recv,
+    d_send, d_recv, e_send, e_recv, local,
 ):
     w = lax.axis_index("wide")
     h = lax.axis_index("heads")
     rows = vq.shape[0]
     half = rows // 2
     few = out_a.shape[0]
+    part_rows, part_few = rows // n, few // n
 
     def place(dw, dh):
         return {"wide": lax.rem(w + dw, n), "heads": lax.rem(h + dh, n)}
@@ -235,7 +247,7 @@
             device_id=device, device_id_type=MESH,
         )
 
-    others = [(dw, dh) for dw in range(n) for dh in range(n) if dw or dh]
+    others = [(d, 0) for d in range(1, n)] + [(0, d) for d in range(1, n)]
     barrier = pltpu.get_barrier_semaphore()
     for dw, dh in others:
         pl.semaphore_signal(barrier, inc=1, device_id=place(dw, dh), device_id_type=MESH)
@@ -297,29 +309,77 @@
     audio = jnp.concatenate(
         [attend(aq, ak, av, HDA, None), attend(caq, cvk, cvv, HDA, wide_bias)], 1
     )
-    for j in range(n):
-        o_rest[j, half:, :] = audio[j * few : (j + 1) * few, :]
-        mixed = attend(p_all[j, :rows, :HDA], cak, cav, HDA, bias_v[j : j + 1, :])
-        o_rest[j, :half, :] = jnp.concatenate([mixed[:half], mixed[half:]], 1)
+    tall_bias = jnp.concatenate(
+        [jnp.broadcast_to(bias_v[j : j + 1, :], (part_rows, bias_v.shape[1])) for j in range(n)], 0
+    )
+    for t in range(n):
+        queries = jnp.concatenate(
+            [p_all[j, t * part_rows : (t + 1) * part_rows, :HDA] for j in range(n)], 0
+        )
+        o_rest[t, half:, :] = jnp.concatenate(
+            [audio[j * few + t * part_few : j * few + (t + 1) * part_few, :] for j in range(n)], 0
+        )
+        mixed = attend(queries, cak, cav, HDA, tall_bias)
+        o_rest[t, :half, :] = jnp.concatenate([mixed[:half], mixed[half:]], 1)
 
     mine = h * n + w
-    b_copies = {}
-
-    def spread(kind, buffer, landing, dh):
-        block = lax.rem(h + dh, n)
-        for dw in range(n):
-            if dw or dh:
-                slot = dw * n + dh
-                copy = remote(
-                    buffer.at[block], landing.at[mine],
-                    b_send.at[kind, slot], b_recv.at[kind, slot], place(dw, dh),
-                )
-                copy.start()
-                b_copies[kind, slot] = copy
-
-    for dh in list(range(1, n)) + [0]:
-        spread(0, o_rest, r_rest, dh)
+    buffers = ((o_rest, r_rest), (o_self, r_self))
+    x_copies = {}
+    steps = n - 1
+
+    def across(kind, d):
+        source, landing = buffers[kind]
+        copy = remote(
+            source.at[lax.rem(h + d, n)], landing.at[mine],
+            x_send.at[kind, d], x_recv.at[kind, d], place(0, d),
+        )
+        copy.start()
+        x_copies[kind, d] = copy
+
+    def along(kind, d, step, way):
+        source, landing = buffers[kind]
+        slot = lax.rem(h + n - d, n) * n + w - way * step
+        piece = source.at[h] if d == 0 and step == 0 else landing.at[slot]
+        at = (((way + 1) // 2 * steps + step) * 2 + kind) * n + d
+        return remote(
+            piece, landing.at[slot], z_send.at[at], z_recv.at[at],
+            {"wide": w + way, "heads": h},
+        )
+
+    def sends(step, way):
+        if way > 0:
+            return (w >= step) & (w < n - 1)
+        return (w + step < n) & (w > 0)
+
+    def forward(kind, d, step):
+        for way in (1, -1):
+            if step:
+                gather(kind, d, step - 1, way)
+
+            @pl.when(sends(step, way))
+            def _():
+                along(kind, d, step, way).start()
+
+    def gather(kind, d, step, way):
+        arrives = (w >= step + 1) if way > 0 else (w + step + 1 < n)
+
+        @pl.when(arrives)
+        def _():
+            landing = buffers[kind][1]
+            at = (((way + 1) // 2 * steps + step) * 2 + kind) * n + d
+            slot = lax.rem(h + n - d, n) * n + w - way * (step + 1)
+            remote(
+                landing.at[slot], landing.at[slot], z_send.at[at], z_recv.at[at],
+                {"wide": w - way, "heads": h},
+            ).wait_recv()
+
+    for d in range(1, n):
+        across(0, d)
+    forward(0, 0, 0)
     r_rest[pl.ds(mine, 1)] = o_rest[pl.ds(h, 1)]
+    for d in range(1, n):
+        x_copies[0, d].wait_recv()
+        forward(0, d, 0)
 
     for i in range(1, 4):
         own[i].wait()
@@ -327,13 +387,23 @@
             a_copies[i, d].wait_recv()
     keys = k_all[...].reshape(n * rows, HDV)
     values = v_all[...].reshape(n * rows, HDV)
-    for dh in list(range(1, n)) + [0]:
-        block = lax.rem(h + dh, n)
-        o_self[pl.ds(block, 1)] = attend(
-            q_all[pl.ds(block, 1)].reshape(rows, HDV), keys, values, HDV, None
-        )[None]
-        spread(1, o_self, r_self, dh)
-    r_self[pl.ds(mine, 1)] = o_self[pl.ds(h, 1)]
+    for d in range(n):
+        block = lax.rem(h + d, n)
+        start = pl.multiple_of(block * part_rows, part_rows)
+        queries = q_all[:, pl.ds(start, part_rows), :].reshape(rows, HDV)
+        o_self[pl.ds(block, 1)] = attend(queries, keys, values, HDV, None)[None]
+        if d:
+            across(1, d)
+        else:
+            forward(1, 0, 0)
+            r_self[pl.ds(mine, 1)] = o_self[pl.ds(h, 1)]
+        if d > 1:
+            x_copies[1, d - 1].wait_recv()
+            forward(1, d - 1, 0)
+        if steps > 1:
+            forward(0, d, 1)
+    x_copies[1, n - 1].wait_recv()
+    forward(1, n - 1, 0)
 
     for copy in w_copies:
         copy.wait_recv()
@@ -344,10 +414,17 @@
             copy.start()
             f_copies.append(copy)
 
+    for kind in range(2):
+        for step in range(2 - kind, steps):
+            for d in range(n):
+                forward(kind, d, step)
+    for kind in range(2):
+        for d in range(n):
+            for way in (1, -1):
+                gather(kind, d, steps - 1, way)
+
     for copy in own[4:]:
         copy.wait()
-    for copy in b_copies.values():
-        copy.wait_recv()
     for copy in f_copies:
         copy.wait_recv()
 
@@ -361,84 +438,130 @@
         0,
     )
     audio_joined = jnp.concatenate([r_rest[s, half:, :] for s in range(heads)], 1)
-    home = {"wide": h, "heads": w}
-    sums = jnp.dot(
-        audio_joined, wa_all[...].reshape(-1, wa.shape[1]), preferred_element_type=jnp.float32
-    )
-    sum_a[...] = sums.astype(jnp.bfloat16)
     width = ws.shape[1] // chunks
-    pieces = [(sum_a, out_a)]
-    last = []
-
-    def deliver(i, source, target):
-        away = remote(source, target, d_send.at[i], d_recv.at[i], home)
-        here = pltpu.make_async_copy(source, target, local.at[7 + i])
-        last.append((away, here))
-
-        @pl.when(w != h)
+    audio_width = wa.shape[1]
+
+    def piece(ref, c):
+        return ref if c == 0 else ref.at[:, (c - 1) * width : c * width]
+
+    def rows_of(ref, c, block):
+        size = part_few if c == 0 else part_rows
+        return piece(ref.at[pl.ds(pl.multiple_of(block * size, size), size)], c)
+
+    def first_hop(c):
+        source, middle = (sum_a, mid_a) if c == 0 else (sum_v, mid_v)
+        for d in range(1, n):
+            copy = remote(
+                rows_of(source, c, lax.rem(w + d, n)), piece(middle.at[w], c),
+                d_send.at[c, d], d_recv.at[c, d], place(d, 0),
+            )
+            copy.start()
+            d_copies[c, d] = copy
+
+    def second_hop(c, d):
+        source, middle, out = (sum_a, mid_a, out_a) if c == 0 else (sum_v, mid_v, out_v)
+        origin = lax.rem(w + n - d, n)
+        ready = piece(middle.at[origin], c) if d else rows_of(source, c, w)
+        target = rows_of(out, c, h)
+        away = remote(
+            ready, target, e_send.at[c, d], e_recv.at[c, lax.rem(origin + n - h, n)],
+            {"wide": w, "heads": origin},
+        )
+        here = pltpu.make_async_copy(ready, target, local.at[7 + c])
+
+        @pl.when(origin != h)
         def _():
             away.start()
 
-        @pl.when(w == h)
+        @pl.when(origin == h)
         def _():
             here.start()
 
-    deliver(0, sum_a, out_a)
-    for c in range(chunks):
-        cols = slice(c * width, (c + 1) * width)
-        sums = jnp.dot(
-            joined, ws_all[:, :, cols].reshape(-1, width), preferred_element_type=jnp.float32
-        ) + jnp.dot(
-            crossed, wc_all[:, :, cols].reshape(-1, width), preferred_element_type=jnp.float32
-        )
-        sum_v[:, cols] = sums.astype(jnp.bfloat16)
-        deliver(1 + c, sum_v.at[:, cols], out_v.at[:, cols])
-
-    @pl.when(w != h)
-    def _():
-        for away, here in last:
-            away.wait()
-
-    @pl.when(w == h)
-    def _():
-        for away, here in last:
+        last.append((origin, away, here))
+
+    d_copies, last = {}, []
+    order = list(range(1, chunks + 1)) + [0]
+    for c in order:
+        if c:
+            cols = slice((c - 1) * width, c * width)
+            sums = jnp.dot(
+                joined, ws_all[:, :, cols].reshape(-1, width), preferred_element_type=jnp.float32
+            ) + jnp.dot(
+                crossed, wc_all[:, :, cols].reshape(-1, width), preferred_element_type=jnp.float32
+            )
+            sum_v[:, cols] = sums.astype(jnp.bfloat16)
+        else:
+            sums = jnp.dot(
+                audio_joined, wa_all[...].reshape(-1, audio_width),
+                preferred_element_type=jnp.float32,
+            )
+            sum_a[...] = sums.astype(jnp.bfloat16)
+        first_hop(c)
+        second_hop(c, 0)
+    for c in order:
+        for d in range(1, n):
+            d_copies[c, d].wait_recv()
+            second_hop(c, d)
+
+    for origin, away, here in last:
+        @pl.when(origin != h)
+        def _():
+            away.wait_send()
+
+        @pl.when(origin == h)
+        def _():
             here.wait()
 
-    for copy in list(a_copies.values()) + w_copies + f_copies + list(b_copies.values()):
+    for c in order:
+        out = out_a if c == 0 else out_v
+        for d in range(1, n):
+            who = lax.rem(h + d, n)
+            target = rows_of(out, c, who)
+            remote(
+                target, target, e_send.at[c, 0], e_recv.at[c, n - d],
+                {"wide": w, "heads": who},
+            ).wait_recv()
+
+    for copy in (
+        list(a_copies.values()) + w_copies + f_copies
+        + list(x_copies.values()) + list(d_copies.values())
+    ):
         copy.wait_send()
+    for step in range(steps):
+        for way in (1, -1):
+            @pl.when(sends(step, way))
+            def _():
+                for kind in range(2):
+                    for d in range(n):
+                        along(kind, d, step, way).wait_send()
 
 
 def shards(*args):
     n = lax.axis_size("wide")
     count = lax.axis_size("heads")
     head_count = args[2].shape[1] // HDV
-    if not (n == count == head_count and n % 2 == 0):
+    if not (n == count == head_count and n % 2 == 0 and args[5].shape[0] % (16 * n) == 0):
         return general_shards(*args)
     (video_hidden, audio_hidden, vq, vk, vv, aq, ak, av, cvq, cak, cav, caq, cvk, cvv,
      vso, vco, aso, aco, table) = args
     rows, few = vq.shape[0], aq.shape[0]
-    blocks = jnp.arange(n, dtype=jnp.int32)
-    offsets = blocks[None, :] - blocks[:, None] + REACH
-    hits = offsets[:, :, None] == jnp.arange(table.shape[1], dtype=jnp.int32)
-    allowed = jnp.any(hits & (table[:, None, :] > 0), axis=2)
-    bias = jnp.where(allowed, 0.0, -1e30).astype(jnp.float32)
-    bias_v = jnp.repeat(bias, few, axis=1)
-    bias_a = jnp.repeat(bias.T, rows, axis=1)
     depth = rows + rows // 2 + 3 * few
     vmem = pl.BlockSpec(memory_space=pltpu.VMEM)
     anywhere = pl.BlockSpec(memory_space=pl.ANY)
     bf16 = jnp.bfloat16
-    pack, wa = pl.pallas_call(
+    pack, wa, bias_v, bias_a = pl.pallas_call(
         functools.partial(pack_kernel, n),
         out_shape=(
             jax.ShapeDtypeStruct((n, depth, 2 * HDA), bf16),
             jax.ShapeDtypeStruct((2 * aso.shape[0], aso.shape[1]), bf16),
+            jax.ShapeDtypeStruct((n, n * few), jnp.float32),
+            jax.ShapeDtypeStruct((n, n * rows), jnp.float32),
         ),
-        in_specs=[vmem] * 11,
-        out_specs=(vmem, vmem),
+        in_specs=[vmem] * 11 + [pl.BlockSpec(memory_space=pltpu.SMEM)],
+        out_specs=(vmem, vmem, vmem, vmem),
         name="pack",
-    )(cvq, cvk, cvv, aq, ak, av, caq, cak, cav, aso, aco)
-    chunks = max(1, vso.shape[1] // 256)
+    )(cvq, cvk, cvv, aq, ak, av, caq, cak, cav, aso, aco, table)
+    chunks = max(1, vso.shape[1] // 512)
     rest = rows // 2 + few
     dma = pltpu.SemaphoreType.DMA
     video_sum, audio_sum = pl.pallas_call(
@@ -463,11 +586,15 @@
             pltpu.VMEM((n * n, rest, 2 * HDA), bf16),
             pltpu.VMEM(video_hidden.shape, bf16),
             pltpu.VMEM(audio_hidden.shape, bf16),
+            pltpu.VMEM((n, rows // n, video_hidden.shape[1]), bf16),
+            pltpu.VMEM((n, few // n, audio_hidden.shape[1]), bf16),
             dma((4, n)), dma((4, n)),
             dma((3, n)), dma((3, n)),
             dma((3, n)), dma((3, n)),
-            dma((2, n * n)), dma((2, n * n)),
-            dma((1 + chunks,)), dma((1 + chunks,)),
+            dma((2, n)), dma((2, n)),
+            dma((4 * n * (n - 1),)), dma((4 * n * (n - 1),)),
+            dma((1 + chunks, n)), dma((1 + chunks, n)),
+            dma((1 + chunks, n)), dma((1 + chunks, n)),
             dma((8 + chunks,)),
         ],
         compiler_params=pltpu.CompilerParams(collective_id=0, has_side_effects=True),

time: 113 us -> 109 us (0.965)
  Pallas kernels: 107 us -> 104 us
  local copies, waits for them, and re-layouts: 1.55 us -> 0.01 us
    pallas_call x1, Pallas kernels: 104 us -> 101 us  [shards(): pl.pallas_call(functools.partial(fused_kernel, n, chunks), out_shape=(jax...]
where the time goes in v2:
time: 109 us; the launch traced here: 107 us
  Pallas kernels  104 us (95%)
  other arithmetic  2.71 us (2%)
    pallas_call x1, Pallas kernels, shards(): pl.pallas_call(functools.partial(fused_kernel, n, chunks), out_shape=(jax...  101 us
    convert_element_type x2, other arithmetic, shards(): return (video_out.astype(bf16), audio_out.astype(bf16))  2.71 us
    pallas_call x1, Pallas kernels, shards(): pl.pallas_call(functools.partial(pack_kernel, n), out_shape=(jax.ShapeDty...  2.52 us

profile of v2, /device:TPU:2, one launch (start us, length us, event | category | flops | bytes accessed | tf_op | source)
XLA Modules:
  0.0 107.3 jit_solution(11375486811509196292)
XLA Ops:
  0.6 2.5 %pack.1 = (bf16[4,576,128]{2,1,0:T(8,128)(2,1)}, bf16[512,512]{1,0:T(8,128)(2,1)}, f32[4,256]{1,0:T(4,128)}, f32[4,1024]{1,0:T(4,128)}) custom-call(bf16[256,256]{1,0:T(8,128)(2,1)} %cvq.1, bf16[256,256]{1,0:T(8,128)(2,1)} %cvk.1, bf16[256,256]{1,0:T(8,128)(2,1)} %cvv.1, bf16[64,256]{1,0:T(8,128)(2,1)} %aq.1, bf16[64,256]{1,0:T(8,128)(2,1)} %ak.1, ...), custom_call_target="tpu_custom_call" | custom-call | tf_op jit(solution)/shard_map/pack/pallas_call | solution.py:552
  3.2 0.0 copy-start
  3.2 101.4 %joint.1 = (bf16[256,1024]{1,0:T(8,128)(2,1)}, bf16[64,512]{1,0:T(8,128)(2,1)}) custom-call(bf16[256,512]{1,0:T(8,128)(2,1)} %vq.1, bf16[256,512]{1,0:T(8,128)(2,1)} %vk.1, bf16[256,512]{1,0:T(8,128)(2,1)} %vv.1, bf16[4,576,128]{2,1,0:T(8,128)(2,1)} %get-tuple-element.8.pack, bf16[512,1024]{1,0:T(8,128)(2,1)} %ws.1, bf16[256,1024]{1,0:T(8,128)(2,1)} %wc.1, ...), custom_call_target="tpu_custom_call" | custom-call | tf_op jit(solution)/shard_map/joint/pallas_call | solution.py:567
  104.6 0.0 copy-done
  104.6 0.0 copy-start.1
  104.6 0.0 copy-start.2
  104.6 2.1 %add_convert_fusion = bf16[256,1024]{1,0:T(8,128)(2,1)} fusion(bf16[256,1024]{1,0:T(8,128)(2,1)} %get-tuple-element.12, bf16[256,1024]{1,0:T(8,128)(2,1)S(1)} %copy-done), kind=kLoop, calls=%fused_computation | loop fusion | flops 1048576 | bytes 1572864 | tf_op jit(solution)/shard_map/convert_element_type | solution.py:605
  106.7 0.0 copy-done.1
  106.7 0.0 copy-done.2
  106.7 0.6 add_convert_fusion.1
Async XLA Ops:
  3.2 101.4 %copy-start = (bf16[256,1024]{1,0:T(8,128)(2,1)S(1)}, bf16[256,1024]{1,0:T(8,128)(2,1)}, u32[]{:S(2)}) copy-start(bf16[256,1024]{1,0:T(8,128)(2,1)} %param.19) | copy-start | bytes 1572868
  104.6 2.1 %copy-start.1 = (bf16[64,512]{1,0:T(8,128)(2,1)S(1)}, bf16[64,512]{1,0:T(8,128)(2,1)}, u32[]{:S(2)}) copy-start(bf16[64,512]{1,0:T(8,128)(2,1)} %param.20) | copy-start | bytes 196612
  104.6 2.1 %copy-start.2 = (bf16[64,512]{1,0:T(8,128)(2,1)S(1)}, bf16[64,512]{1,0:T(8,128)(2,1)}, u32[]{:S(2)}) copy-start(bf16[64,512]{1,0:T(8,128)(2,1)} %get-tuple-element.13) | copy-start | bytes 196612

commit v3 on v2

--- a/solution.py
+++ b/solution.py
@@ -275,15 +275,34 @@
 
     pairs = ((ws, ws_all), (wc, wc_all), (wa, wa_all))
     partner = {"wide": w, "heads": h + 1 - 2 * lax.rem(h, 2)}
-    w_copies, f_copies = [], []
-    for i, (source, target) in enumerate(pairs):
+    w_copies, f_copies = [[], [], []], [[], [], []]
+
+    def send_weights(i):
+        source, target = pairs[i]
         for k in range(1, n // 2):
             copy = remote(source, target.at[h], w_send.at[i, k], w_recv.at[i, k], place(0, 2 * k))
             copy.start()
-            w_copies.append(copy)
+            w_copies[i].append(copy)
+
+    def pass_weights(i):
+        target = pairs[i][1]
+        for k in range(1, n // 2):
+            w_copies[i][k - 1].wait_recv()
+            slot = lax.rem(h + n - 2 * k, n)
+            copy = remote(target.at[slot], target.at[slot], f_send.at[i, k], f_recv.at[i, k], partner)
+            copy.start()
+            f_copies[i].append(copy)
+
+    def settle_weights(i):
+        own[4 + i].wait()
+        for copy in f_copies[i]:
+            copy.wait_recv()
+
+    send_weights(0)
+    for i, (source, target) in enumerate(pairs):
         copy = remote(source, target.at[h], f_send.at[i, 0], f_recv.at[i, 0], partner)
         copy.start()
-        f_copies.append(copy)
+        f_copies[i].append(copy)
 
     own[0].wait()
     for d in range(1, n):
@@ -375,6 +394,7 @@
 
     for d in range(1, n):
         across(0, d)
+    send_weights(1)
     forward(0, 0, 0)
     r_rest[pl.ds(mine, 1)] = o_rest[pl.ds(h, 1)]
     for d in range(1, n):
@@ -405,14 +425,9 @@
     x_copies[1, n - 1].wait_recv()
     forward(1, n - 1, 0)
 
-    for copy in w_copies:
-        copy.wait_recv()
-    for i, (source, target) in enumerate(pairs):
-        for k in range(1, n // 2):
-            slot = lax.rem(h + n - 2 * k, n)
-            copy = remote(target.at[slot], target.at[slot], f_send.at[i, k], f_recv.at[i, k], partner)
-            copy.start()
-            f_copies.append(copy)
+    send_weights(2)
+    pass_weights(0)
+    pass_weights(1)
 
     for kind in range(2):
         for step in range(2 - kind, steps):
@@ -423,10 +438,9 @@
             for way in (1, -1):
                 gather(kind, d, steps - 1, way)
 
-    for copy in own[4:]:
-        copy.wait()
-    for copy in f_copies:
-        copy.wait_recv()
+    pass_weights(2)
+    settle_weights(0)
+    settle_weights(1)
 
     heads = n * n
     joined = jnp.concatenate([r_self[s] for s in range(heads)], 1)
@@ -491,6 +505,7 @@
             )
             sum_v[:, cols] = sums.astype(jnp.bfloat16)
         else:
+            settle_weights(2)
             sums = jnp.dot(
                 audio_joined, wa_all[...].reshape(-1, audio_width),
                 preferred_element_type=jnp.float32,
@@ -523,7 +538,7 @@
             ).wait_recv()
 
     for copy in (
-        list(a_copies.values()) + w_copies + f_copies
+        list(a_copies.values()) + sum(w_copies, []) + sum(f_copies, [])
         + list(x_copies.values()) + list(d_copies.values())
     ):
         copy.wait_send()

time: 109 us -> 93.2 us (0.86)
  Pallas kernels: 104 us -> 88.4 us
    pallas_call x1, Pallas kernels: 101 us -> 85.9 us  [shards(): pl.pallas_call(functools.partial(fused_kernel, n, chunks), out_shape=(jax...]
where the time goes in v3:
time: 93.2 us; the launch traced here: 91.8 us
  Pallas kernels  88.4 us (95%)
  other arithmetic  2.71 us (3%)
    pallas_call x1, Pallas kernels, shards(): pl.pallas_call(functools.partial(fused_kernel, n, chunks), out_shape=(jax...  85.9 us
    convert_element_type x2, other arithmetic, shards(): return (video_out.astype(bf16), audio_out.astype(bf16))  2.71 us
    pallas_call x1, Pallas kernels, shards(): pl.pallas_call(functools.partial(pack_kernel, n), out_shape=(jax.ShapeDty...  2.52 us

profile of v3, /device:TPU:2, one launch (start us, length us, event | category | flops | bytes accessed | tf_op | source)
XLA Modules:
  0.0 91.8 jit_solution(11698880009314394108)
XLA Ops:
  0.6 2.5 %pack.1 = (bf16[4,576,128]{2,1,0:T(8,128)(2,1)}, bf16[512,512]{1,0:T(8,128)(2,1)}, f32[4,256]{1,0:T(4,128)}, f32[4,1024]{1,0:T(4,128)}) custom-call(bf16[256,256]{1,0:T(8,128)(2,1)} %cvq.1, bf16[256,256]{1,0:T(8,128)(2,1)} %cvk.1, bf16[256,256]{1,0:T(8,128)(2,1)} %cvv.1, bf16[64,256]{1,0:T(8,128)(2,1)} %aq.1, bf16[64,256]{1,0:T(8,128)(2,1)} %ak.1, ...), custom_call_target="tpu_custom_call" | custom-call | tf_op jit(solution)/shard_map/pack/pallas_call | solution.py:567
  3.2 0.0 copy-start
  3.2 85.9 %joint.1 = (bf16[256,1024]{1,0:T(8,128)(2,1)}, bf16[64,512]{1,0:T(8,128)(2,1)}) custom-call(bf16[256,512]{1,0:T(8,128)(2,1)} %vq.1, bf16[256,512]{1,0:T(8,128)(2,1)} %vk.1, bf16[256,512]{1,0:T(8,128)(2,1)} %vv.1, bf16[4,576,128]{2,1,0:T(8,128)(2,1)} %get-tuple-element.8.pack, bf16[512,1024]{1,0:T(8,128)(2,1)} %ws.1, bf16[256,1024]{1,0:T(8,128)(2,1)} %wc.1, ...), custom_call_target="tpu_custom_call" | custom-call | tf_op jit(solution)/shard_map/joint/pallas_call | solution.py:582
  89.1 0.0 copy-done
  89.1 0.0 copy-start.1
  89.1 0.0 copy-start.2
  89.1 2.1 %add_convert_fusion = bf16[256,1024]{1,0:T(8,128)(2,1)} fusion(bf16[256,1024]{1,0:T(8,128)(2,1)} %get-tuple-element.12, bf16[256,1024]{1,0:T(8,128)(2,1)S(1)} %copy-done), kind=kLoop, calls=%fused_computation | loop fusion | flops 1048576 | bytes 1572864 | tf_op jit(solution)/shard_map/convert_element_type | solution.py:620
  91.2 0.0 copy-done.1
  91.2 0.0 copy-done.2
  91.2 0.6 add_convert_fusion.1
Async XLA Ops:
  3.2 85.9 %copy-start = (bf16[256,1024]{1,0:T(8,128)(2,1)S(1)}, bf16[256,1024]{1,0:T(8,128)(2,1)}, u32[]{:S(2)}) copy-start(bf16[256,1024]{1,0:T(8,128)(2,1)} %param.19) | copy-start | bytes 1572868
  89.1 2.1 %copy-start.1 = (bf16[64,512]{1,0:T(8,128)(2,1)S(1)}, bf16[64,512]{1,0:T(8,128)(2,1)}, u32[]{:S(2)}) copy-start(bf16[64,512]{1,0:T(8,128)(2,1)} %param.20) | copy-start | bytes 196612
  89.1 2.1 %copy-start.2 = (bf16[64,512]{1,0:T(8,128)(2,1)S(1)}, bf16[64,512]{1,0:T(8,128)(2,1)}, u32[]{:S(2)}) copy-start(bf16[64,512]{1,0:T(8,128)(2,1)} %get-tuple-element.13) | copy-start | bytes 196612
